TPU v7x, 32 devices: a whole 2x2x4 slice. The times are simulated.
32 devices in a mesh: chan: 8 (over y, x, core), grp: 4 (over z).
Axes of the slice: x: 2, y: 2, z: 4, core: 2. Of those that a mesh axis runs over, the one named last changes fastest.
Arguments:
- raw_files: float32 [4, 2048, 1024], P('grp', 'chan'), may hold values from -6 to 6
- file_target: int32 [4, 2048], P('grp', 'chan'), may hold values from -1 to 511, as said below
- file_len: int32 [4, 2048], P('grp', 'chan'), may hold values from 768 to 1024
- fir_taps: float32 [64], replicated, may hold values from -0.75 to 0.75
- source_slot: int32 [8], replicated, may hold values from 0 to 15
Outputs:
- stacks: bfloat16 [8, 128, 256], P('grp', 'chan')
Inputs may be any that keep to these rules, and one draw needn't show every extreme that they name: `file_target`: -1 marks an empty slot; any other entry o * 64 + j names file j of owner o, which holds channel o * 16 + j // 4, window (j // 2) % 2 and half j % 2 of that window. For each grp index every file of every owner stands in exactly one slot, so every owner receives exactly 64 files; a reader holds either none or exactly 32 files of one owner; some reader holds 256 files.
All inputs are finite; a program needn't handle non-finite values.
Results may differ from a plain program's by a relative error of at most 0.017.
Values may be sent and summed in bfloat16 or wider, within the bound.
A program may use at most 64 MiB of HBM per device.

v0:
```python
import math

import jax
import jax.numpy as jnp
from jax import lax
from jax.sharding import PartitionSpec as P

CB = 16
WINS = 2
WIN = 512
DEC = 4
TAPS = 64
LAGS = 256
ENVW = 64


ENVELOPE_FLOOR = 0.3
lag_step = 16


def shortened(array):
    return jax.tree.map(lambda a: a.astype(jnp.bfloat16) if a.dtype == jnp.float32 else a, array)


def decimate(samples, lengths, fir_taps):
    sample_count = samples.shape[-1]
    trimmed = jnp.where(
        jnp.arange(sample_count, dtype=jnp.int32) < lengths[:, None],
        samples,
        jnp.zeros_like(samples),
    )
    kernel = fir_taps[::-1].reshape(1, 1, TAPS)
    filtered = lax.conv_general_dilated(
        trimmed[:, None, :], kernel, (DEC,), [(TAPS - 1, 0)], precision=lax.Precision.HIGHEST
    )
    return filtered[:, 0, :]


def normalize(trace_rows):
    row_ids = jnp.arange(WIN, dtype=jnp.int32)[:, None]
    column_ids = jnp.arange(WIN, dtype=jnp.int32)[None, :]
    inside = (column_ids - row_ids >= -(ENVW // 2)) & (column_ids - row_ids < ENVW // 2)
    window_band = jnp.where(inside, 1.0 / ENVW, 0.0).astype(jnp.float32)
    envelope = jnp.dot(jnp.abs(trace_rows), window_band.T, precision=lax.Precision.HIGHEST)
    return (trace_rows / jnp.maximum(envelope, ENVELOPE_FLOOR)).astype(jnp.bfloat16)


def shifted_receivers(receivers):
    lag_half = LAGS // 2
    channel_count, window_count, _ = receivers.shape
    span_len = window_count * (WIN + lag_half)
    flattened = jnp.pad(receivers, ((0, 0), (0, 0), (0, lag_half))).reshape(channel_count, span_len)
    widened = jnp.pad(flattened, ((0, 0), (lag_step, 0)))
    copies = [
        lax.slice_in_dim(widened, lag_step - offset, lag_step - offset + span_len, 1, 1)
        for offset in range(lag_step)
    ]
    return jnp.stack(copies).reshape(lag_step * channel_count, span_len)


def correlate(shifted, sources, own_first, source_slot, stack_scale):
    lag_half = LAGS // 2
    row_count = sources.shape[0]
    channel_count = shifted.shape[0] // lag_step
    span_len = shifted.shape[1]
    window_count = span_len // (WIN + lag_half)
    padded = jnp.pad(sources.reshape(row_count, window_count, WIN), ((0, 0), (0, 0), (0, lag_half)))
    padded = jnp.pad(padded.reshape(row_count, span_len), ((0, 0), (lag_half, lag_half)))
    blocks = []
    for lag_block in range(LAGS // lag_step):
        window_view = lax.slice_in_dim(
            padded, lag_block * lag_step, lag_block * lag_step + span_len, 1, 1
        )
        blocks.append(
            lax.dot_general(
                window_view, shifted, (((1,), (1,)), ((), ())), preferred_element_type=jnp.float32
            )
        )
    result = jnp.stack(blocks, axis=1).reshape(row_count, LAGS // lag_step, lag_step, channel_count)
    result = jnp.transpose(result, (0, 3, 1, 2)).reshape(row_count, channel_count, LAGS)
    owners = jnp.arange(row_count, dtype=jnp.int32)
    source_channel = owners * CB + source_slot
    receiver_channel = own_first + jnp.arange(channel_count, dtype=jnp.int32)
    distinct = source_channel[:, None] != receiver_channel[None, :]
    return jnp.where(distinct[:, :, None], result * stack_scale, 0.0)


def local(raw_files, file_target, file_len, fir_taps, source_slot):
    owner_count = lax.axis_size("chan")
    group_count = lax.axis_size("grp")
    slot_count = raw_files.shape[1]
    capacity = slot_count // owner_count
    file_count = 2 * CB * WINS
    targets = file_target[0]
    owner_of = jnp.where(targets >= 0, targets // file_count, -1)
    local_id = jnp.where(targets >= 0, targets % file_count, -1)
    positions = jnp.arange(slot_count, dtype=jnp.int32)
    earlier = (owner_of[None, :] == owner_of[:, None]) & (positions[None, :] < positions[:, None])
    slot_rank = jnp.sum(earlier.astype(jnp.int32), axis=1)
    slot_index = jnp.where(targets >= 0, owner_of * capacity + slot_rank, slot_count)

    def pack_slots(values, fill_value):
        buffer = (
            jnp.full((slot_count,) + values.shape[1:], fill_value, values.dtype)
            .at[slot_index]
            .set(values, mode="drop")
        )
        return buffer.reshape((owner_count, capacity) + values.shape[1:])

    ids_packed = pack_slots(local_id, -1)
    filtered = decimate(raw_files[0], file_len[0], fir_taps)
    received, received_ids = (
        lax.all_to_all(
            shortened(pack_slots(filtered, 0.0)), "chan", split_axis=0, concat_axis=0, tiled=True
        ),
        lax.all_to_all(ids_packed, "chan", split_axis=0, concat_axis=0, tiled=True),
    )
    half_len = received.shape[-1]
    destination = received_ids.reshape(-1)
    destination = jnp.where(destination < 0, file_count, destination)
    placed = (
        jnp.zeros((file_count, half_len), jnp.float32)
        .at[destination]
        .set(received.reshape(-1, half_len), mode="drop")
    )
    traces = normalize(placed.reshape(CB * WINS, WIN)).reshape(CB, WINS, WIN)
    stack_scale = 1.0 / math.sqrt(group_count * WINS * WIN)
    chan_index = lax.axis_index("chan")
    own_slot = lax.dynamic_slice_in_dim(source_slot, chan_index, 1)[0]
    own_source = lax.dynamic_slice_in_dim(traces, own_slot, 1, 0).reshape(1, WINS * WIN)
    own_first = chan_index * CB
    shifted = shifted_receivers(traces)
    term_rows = correlate(
        shifted,
        lax.all_gather(own_source, "chan", axis=0, tiled=True),
        own_first,
        source_slot,
        stack_scale,
    )
    stacks = lax.psum_scatter(
        term_rows.astype(jnp.bfloat16), "grp", scatter_dimension=0, tiled=True
    )
    return stacks


def solution(mesh):
    placed = (P("grp", "chan", None), P("grp", "chan"), P("grp", "chan"), P(), P())
    return jax.shard_map(
        local, mesh=mesh, in_specs=placed, out_specs=P("grp", "chan", None), check_vma=False
    )
```

profile of v0, /device:TPU:0, one launch (start us, length us, event | category | flops | bytes accessed | tf_op | source)
XLA Modules:
  0.0 109.9 jit_solution(10314538478814102478)
XLA Ops:
  6.5 0.7 compare_select_fusion.3
  7.2 0.7 copy-done
  7.9 0.2 convert_reduce_fusion
  8.1 1.4 %scatter_custom_fusion = s32[256]{0:T(256)S(1)} fusion(s32[256]{0:T(256)S(1)} %bitcast.229, s32[256]{0:T(256)S(1)} %get-tuple-element.7, s32[]{:T(128)} %constant.23.clone.1), kind=kCustom, calls=%fused_computation.150 | custom fusion | bytes 1028 | tf_op jit(solution)/shard_map/scatter | solution.py:106
  9.5 0.7 all_to_all.9
  10.2 5.2 %all-to-all-start = ((s32[8,1,32]{2,1,0:T(1,128)}), s32[8,1,32]{2,1,0:T(1,128)S(1)}, u32[]{:S(2)}, u32[]{:S(2)}) async-start(s32[8,1,32]{2,1,0:T(1,128)} %all_to_all.9), calls=%async_computation | async-start | bytes 8192 | tf_op jit(solution)/shard_map/all_to_all | solution.py:116
  15.4 0.7 copy-done.1
  16.1 1.4 %bitcast_select_fusion = f32[256,1,1024]{2,0,1:T(8,128)S(1)} fusion(f32[1,256,1024]{2,1,0:T(8,128)} %param.5, s32[256]{0:T(256)S(1)} %bitcast.228), kind=kLoop, calls=%fused_computation.38 | loop fusion | flops 524288 | bytes 2098176 | tf_op jit(solution)/shard_map/jit(_where)/select_n | solution.py:27
  17.5 0.8 copy.17
  18.2 0.1 rev.3
  18.3 0.1 copy.18
  18.5 0.6 copy-done.3
  19.1 21.9 %fusion.107 = f32[256,1,256]{0,1,2:T(1,128)S(1)} fusion(f32[256,1,1024]{0,1,2:T(1,128)S(1)} %copy.17, f32[1,1,64]{1,0,2:T(1,128)S(1)} %copy.18), kind=kOutput, calls=%fused_computation.176 | convolution fusion | flops 48709632 | bytes 1310976 | tf_op jit(solution)/shard_map/conv_general_dilated | solution.py:33
  41.0 0.1 broadcast_compare_fusion
  41.1 0.6 dynamic_slice.6
  42.8 0.1 copy.21
  42.9 1.5 %scatter_custom_fusion.1 = f32[256,256]{1,0:T(8,128)S(1)} fusion(s32[256]{0:T(256)S(1)} %bitcast.230, f32[256,1,256]{2,0,1:T(8,128)S(1)} %copy.21, f32[]{:T(128)} %constant.22.clone.1), kind=kCustom, calls=%fused_computation.52 | custom fusion | bytes 524292 | tf_op jit(solution)/shard_map/scatter | solution.py:106
  44.5 0.7 convert_element_type.30
  45.7 4.2 %all-to-all-start.1 = ((bf16[8,32,256]{2,1,0:T(8,128)(2,1)}), bf16[8,32,256]{2,1,0:T(8,128)(2,1)S(1)}, u32[]{:S(2)}, u32[]{:S(2)}) async-start(bf16[8,32,256]{2,1,0:T(8,128)(2,1)} %bitcast.10), calls=%async_computation.1 | async-start | bytes 262144 | tf_op jit(solution)/shard_map/all_to_all | solution.py:113
  49.9 0.0 reduce-scatter.2.cloned.1.call-start
  49.9 0.5 broadcast.264
  50.5 0.7 reduce.4
  51.1 0.1 reshape.375
  51.2 4.2 %all-to-all-done.1 = bf16[8,32,256]{2,1,0:T(8,128)(2,1)S(1)} async-done(((bf16[8,32,256]{2,1,0:T(8,128)(2,1)}), bf16[8,32,256]{2,1,0:T(8,128)(2,1)S(1)}, u32[]{:S(2)}, u32[]{:S(2)}) %all-to-all-start.1) | async-done | bytes 131104 | tf_op jit(solution)/shard_map/all_to_all | solution.py:113
  55.4 1.5 %scatter_custom_fusion.2 = f32[64,256]{1,0:T(8,128)S(1)} fusion(s32[256]{0:T(256)S(1)} %bitcast.231, bf16[256,256]{1,0:T(8,128)(2,1)S(1)} %bitcast.223, f32[]{:T(128)} %constant.22.clone.1), kind=kCustom, calls=%fused_computation.50 | custom fusion | flops 65536 | bytes 196612 | tf_op jit(solution)/shard_map/scatter | solution.py:124
  56.9 0.8 fusion.17
  57.9 0.1 constant_dynamic-update-slice_fusion.14
  57.9 0.1 constant_dynamic-update-slice_fusion.13
  58.0 0.1 constant_dynamic-update-slice_fusion.12
  58.1 0.1 constant_dynamic-update-slice_fusion.11
  58.2 0.1 constant_dynamic-update-slice_fusion.10
  58.3 0.1 constant_dynamic-update-slice_fusion.9
  58.4 0.1 constant_dynamic-update-slice_fusion.8
  58.4 0.1 constant_dynamic-update-slice_fusion.7
  58.5 0.1 constant_dynamic-update-slice_fusion.6
  58.6 0.1 constant_dynamic-update-slice_fusion.5
  58.7 0.1 constant_dynamic-update-slice_fusion.4
  58.8 0.1 constant_dynamic-update-slice_fusion.3
  58.9 0.1 constant_dynamic-update-slice_fusion.2
  58.9 0.1 constant_dynamic-update-slice_fusion.1
  59.0 0.1 constant_dynamic-update-slice_fusion
  59.1 8.3 %all-gather = bf16[8,1,1024]{2,1,0:T(2,128)(2,1)S(1)} all-gather(bf16[1,1,1024]{2,1,0:T(2,128)(2,1)S(1)} %reshape.408), channel_id=1, replica_groups=mesh['chan'=8,'grp'=4] {'chan'}, dimensions={0}, use_global_device_ids=true | all-gather | bytes 18432 | tf_op jit(solution)/shard_map/all_gather | solution.py:135
  67.5 0.1 reduce.1
  67.6 0.9 fusion.15
  68.5 0.9 fusion.14
  69.4 0.9 fusion.13
  70.3 0.9 fusion.12
  71.2 0.9 fusion.11
  72.1 0.9 fusion.10
  73.0 0.9 fusion.9
  73.9 0.9 fusion.8
  74.9 0.9 fusion.7
  75.7 0.9 fusion.6
  76.7 0.9 fusion.5
  77.6 0.9 fusion.4
  78.5 0.9 fusion.3
  79.4 0.9 fusion.2
  80.3 0.9 fusion.1
  81.2 0.9 fusion
  82.1 0.1 broadcast_multiply_fusion
  82.2 0.3 copy.20
  82.6 0.7 select_convert_fusion
  83.3 0.0 reduce-scatter.2.cloned.1.call-update
  83.3 19.8 %reduce-scatter.2.cloned.1.call-done = bf16[2,16,256]{2,1,0:T(8,128)(2,1)} async-done(((bf16[8,16,256]{2,1,0:T(8,128)(2,1)}), bf16[2,16,256]{2,1,0:T(8,128)(2,1)}) %reduce-scatter.2.cloned.1.call-update) | async-done | bytes 16400 | tf_op jit(solution)/shard_map/reduce_scatter | solution.py:140
  (23 shorter events, 0.3 us)
Async XLA Ops:
  7.2 0.7 copy-start
  10.2 35.5 %all-to-all-start = ((s32[8,1,32]{2,1,0:T(1,128)}), s32[8,1,32]{2,1,0:T(1,128)S(1)}, u32[]{:S(2)}, u32[]{:S(2)}) async-start(s32[8,1,32]{2,1,0:T(1,128)} %all_to_all.9), calls=%async_computation | async-start | bytes 8192 | tf_op jit(solution)/shard_map/all_to_all | solution.py:116
  15.4 0.7 copy-start.1
  17.4 0.8 copy-start.2
  18.4 0.7 copy-start.3
  45.7 9.7 %all-to-all-start.1 = ((bf16[8,32,256]{2,1,0:T(8,128)(2,1)}), bf16[8,32,256]{2,1,0:T(8,128)(2,1)S(1)}, u32[]{:S(2)}, u32[]{:S(2)}) async-start(bf16[8,32,256]{2,1,0:T(8,128)(2,1)} %bitcast.10), calls=%async_computation.1 | async-start | bytes 262144 | tf_op jit(solution)/shard_map/all_to_all | solution.py:113
  49.9 53.2 %reduce-scatter.2.cloned.1.call-start = ((), (), s32[]{:S(2)}) async-start(), calls=%async_computation.3 | async-start | bytes 81920 | tf_op jit(solution)/shard_map/reduce_scatter | solution.py:140
Sparse Core Ops, SparseCore 0:
  83.4 19.5 reduce-scatter.1
where the time goes:
time: 110 us
  matrix products  37.2 us (34%)
  waiting for transfers between devices  24 us (22%)
  between operations  15.3 us (14%)
  local copies, waits for them, and re-layouts  9.63 us (9%)
  starting transfers between devices  9.45 us (9%)
  blocking collectives  8.35 us (8%)
  other arithmetic  6.04 us (5%)
    conv_general_dilated x1, matrix products, decimate(): lax.conv_general_dilated(trimmed[:, None, :], kernel, (DEC,), [(TAPS - 1,...  21.9 us
    reduce_scatter x1, waiting for transfers between devices, local(): lax.psum_scatter(term_rows.astype(jnp.bfloat16), 'grp', scatter_dimension...  19.8 us
    dot_general x16, matrix products, correlate(): lax.dot_general(window_view, shifted, (((1,), (1,)), ((), ())), preferred...  14.4 us
    all_gather x1, blocking collectives, local(): lax.all_gather(own_source, 'chan', axis=0, tiled=True)  8.35 us
    all_to_all x1, starting transfers between devices, local(): lax.all_to_all(ids_packed, 'chan', split_axis=0, concat_axis=0, tiled=True)  5.2 us
    all_to_all x1, starting transfers between devices, local(): lax.all_to_all(shortened(pack_slots(filtered, 0.0)), 'chan', split_axis=0...  4.21 us
    all_to_all x1, waiting for transfers between devices, local(): lax.all_to_all(shortened(pack_slots(filtered, 0.0)), 'chan', split_axis=0...  4.19 us
    unnamed x26, local copies, waits for them, and re-layouts  3.2 us
  transfers between devices with their start and end apart: 3, of which 2 were waited for; matrix products, arithmetic and copies ran while one was open for 26% of the time, Pallas kernels for 0%

commit v1 on v0

--- a/solution.py
+++ b/solution.py
@@ -1,8 +1,11 @@
+import functools
 import math
 
 import jax
 import jax.numpy as jnp
 from jax import lax
+from jax.experimental import pallas as pl
+from jax.experimental.pallas import tpu as pltpu
 from jax.sharding import PartitionSpec as P
 
 CB = 16
@@ -143,8 +146,209 @@
     return stacks
 
 
+def iota(shape, dim):
+    return lax.broadcasted_iota(jnp.int32, shape, dim)
+
+
+def column_of(row):
+    count = row.shape[1]
+    square = (count, count)
+    return jnp.sum(jnp.where(iota(square, 0) == iota(square, 1), row, 0.0), axis=1, keepdims=True)
+
+
+def fir_matrix(taps_row):
+    taps_column = column_of(taps_row)
+    spread = (TAPS, 128)
+    reverse = jnp.sum(
+        jnp.where(iota(spread, 0) + iota(spread, 1) == TAPS - 1, taps_column, 0.0), axis=0, keepdims=True
+    )
+    raw_len = 1024
+    half_len = raw_len // DEC
+    wide = jnp.concatenate([reverse, jnp.zeros((1, raw_len - 128), jnp.float32)], axis=1)
+    wide = jnp.broadcast_to(wide, (8, raw_len))
+    block = pltpu.roll(wide, raw_len - TAPS + 1, 1, stride=DEC, stride_axis=0)
+    rows = [block if i == 0 else pltpu.roll(block, 8 * DEC * i, 1) for i in range(half_len // 8)]
+    matrix = jnp.concatenate(rows, axis=0)
+    return jnp.where(iota(matrix.shape, 1) <= DEC * iota(matrix.shape, 0), matrix, 0.0)
+
+
+def split(values):
+    high = values.astype(jnp.bfloat16)
+    return high, (values - high.astype(jnp.float32)).astype(jnp.bfloat16)
+
+
+def dot_rows(a, b):
+    return lax.dot_general(a, b, (((1,), (1,)), ((), ())), preferred_element_type=jnp.float32)
+
+
+def dot(a, b):
+    return jnp.dot(a, b, preferred_element_type=jnp.float32)
+
+
+def kernel(
+    owner_count, group_count, stack_scale,
+    raw_ref, target_ref, len_ref, taps_ref, slot_ref, out_ref,
+    files, arrived, own_source, sources, terms, sums, band_ref, flip_ref,
+    file_send, file_recv, source_send, source_recv, sum_send, sum_recv,
+):
+    me = lax.axis_index("chan")
+    group = lax.axis_index("grp")
+    slot_count = raw_ref.shape[1]
+    file_count = 2 * CB * WINS
+    per_group = owner_count // group_count
+    lag_half = LAGS // 2
+
+    barrier = pltpu.get_barrier_semaphore()
+    for step in range(1, owner_count):
+        pl.semaphore_signal(
+            barrier, inc=1, device_id={"chan": lax.rem(me + step, owner_count)}, device_id_type=pl.DeviceIdType.MESH
+        )
+    for step in range(1, group_count):
+        pl.semaphore_signal(
+            barrier, inc=1, device_id={"grp": lax.rem(group + step, group_count)}, device_id_type=pl.DeviceIdType.MESH
+        )
+
+    lengths = column_of(len_ref[...].astype(jnp.float32)).astype(jnp.int32)
+    raw = raw_ref[0]
+    trimmed = jnp.where(iota(raw.shape, 1) < lengths, raw, 0.0)
+    raw_high, raw_low = split(trimmed)
+    fir_high, fir_low = split(fir_matrix(taps_ref[...]))
+    filtered = dot_rows(raw_high, fir_high) + (dot_rows(raw_low, fir_high) + dot_rows(raw_high, fir_low))
+    filtered = filtered.astype(jnp.bfloat16)
+
+    shape = (owner_count * file_count, slot_count)
+    place = iota(shape, 0)
+    within = place % file_count
+    wanted = (
+        place - within
+        + 2 * (2 * (within % CB) + (within // CB) % WINS)
+        + within // (CB * WINS)
+    )
+    pick = jnp.where(wanted == target_ref[...], 1.0, 0.0).astype(jnp.bfloat16)
+    files[...] = dot(pick, filtered).astype(jnp.bfloat16).reshape(files.shape)
+
+    pl.semaphore_wait(barrier, owner_count + group_count - 2)
+
+    def to_owner(step, source, landing, send, recv):
+        return pltpu.make_async_remote_copy(
+            src_ref=source, dst_ref=landing, send_sem=send.at[step - 1], recv_sem=recv.at[step - 1],
+            device_id={"chan": lax.rem(me + step, owner_count)}, device_id_type=pl.DeviceIdType.MESH,
+        )
+
+    file_copies = [
+        to_owner(step, files.at[lax.rem(me + step, owner_count)], arrived.at[step - 1], file_send, file_recv)
+        for step in range(1, owner_count)
+    ]
+    for copy in file_copies:
+        copy.start()
+    square = (WIN, WIN)
+    ahead = iota(square, 0) - iota(square, 1)
+    inside = (ahead >= -(ENVW // 2)) & (ahead < ENVW // 2)
+    band_ref[...] = jnp.where(inside, 1.0 / ENVW, 0.0).astype(jnp.bfloat16)
+    mirrored = iota(square, 0) + iota(square, 1) == WIN - 1
+    flip_ref[...] = jnp.where(mirrored, 1.0, 0.0).astype(jnp.bfloat16)
+    placed = files[me].astype(jnp.float32)
+    for step, copy in enumerate(file_copies):
+        copy.wait_recv()
+        placed = placed + arrived[step].astype(jnp.float32)
+
+    rows = CB * WINS
+    trace = jnp.concatenate([placed[:rows], placed[rows:]], axis=1)
+    envelope = dot(jnp.abs(trace).astype(jnp.bfloat16), band_ref[...])
+    normal = trace / jnp.maximum(envelope, ENVELOPE_FLOOR)
+    chosen = iota((CB, 1), 0) == slot_ref[me]
+    own = jnp.concatenate(
+        [
+            jnp.sum(jnp.where(chosen, normal[w * CB:(w + 1) * CB], 0.0), axis=0, keepdims=True)
+            for w in range(WINS)
+        ],
+        axis=1,
+    )
+    own_source[...] = own
+    sources[me] = own
+    source_copies = [
+        to_owner(step, own_source, sources.at[me], source_send, source_recv) for step in range(1, owner_count)
+    ]
+    for copy in source_copies:
+        copy.start()
+    flipped = dot(normal.astype(jnp.bfloat16), flip_ref[...]).astype(jnp.bfloat16)
+    receivers = jnp.concatenate([flipped[w * CB:(w + 1) * CB] for w in range(WINS)], axis=1)
+    for copy in source_copies:
+        copy.wait_recv()
+
+    def correlation(owner):
+        source = sources[owner].astype(jnp.bfloat16).astype(jnp.float32)
+        pieces = []
+        for w in range(WINS):
+            row = jnp.concatenate(
+                [source[:, w * WIN:(w + 1) * WIN], jnp.zeros((1, LAGS), jnp.float32)], axis=1
+            )
+            row = jnp.broadcast_to(row, (lag_half, WIN + LAGS))
+            shifted = pltpu.roll(row, 1, 1, stride=1, stride_axis=0).astype(jnp.bfloat16)
+            for begin in range(WIN - 128, -1, -128):
+                pieces.append(shifted[:, begin:begin + LAGS])
+        result = dot(receivers, jnp.concatenate(pieces, axis=0)) * stack_scale
+        own_row = iota((CB, 1), 0) + me * CB == owner * CB + slot_ref[owner]
+        return jnp.where(own_row, 0.0, result).astype(jnp.bfloat16)
+
+    sum_copies = []
+    for step in list(range(1, group_count)) + [0]:
+        peer = lax.rem(group + step, group_count)
+        for index in range(per_group):
+            terms[step, index] = correlation(peer * per_group + index)
+        if step:
+            copy = pltpu.make_async_remote_copy(
+                src_ref=terms.at[step], dst_ref=sums.at[step - 1],
+                send_sem=sum_send.at[step - 1], recv_sem=sum_recv.at[step - 1],
+                device_id={"grp": peer}, device_id_type=pl.DeviceIdType.MESH,
+            )
+            copy.start()
+            sum_copies.append(copy)
+    total = terms[0].astype(jnp.float32)
+    for step, copy in enumerate(sum_copies):
+        copy.wait_recv()
+        total = total + sums[step].astype(jnp.float32)
+    out_ref[...] = total.astype(jnp.bfloat16)
+    for copy in file_copies + source_copies + sum_copies:
+        copy.wait_send()
+
+
+def fused(raw_files, file_target, file_len, fir_taps, source_slot):
+    owner_count = lax.axis_size("chan")
+    group_count = lax.axis_size("grp")
+    file_count = 2 * CB * WINS
+    half_len = raw_files.shape[2] // DEC
+    per_group = owner_count // group_count
+    stack_scale = 1.0 / math.sqrt(group_count * WINS * WIN)
+    vmem = pl.BlockSpec(memory_space=pltpu.VMEM)
+    dma = pltpu.SemaphoreType.DMA
+    return pl.pallas_call(
+        functools.partial(kernel, owner_count, group_count, stack_scale),
+        out_shape=jax.ShapeDtypeStruct((per_group, CB, LAGS), jnp.bfloat16),
+        in_specs=[vmem] * 4 + [pl.BlockSpec(memory_space=pltpu.SMEM)],
+        out_specs=vmem,
+        scratch_shapes=[
+            pltpu.VMEM((owner_count, file_count, half_len), jnp.bfloat16),
+            pltpu.VMEM((owner_count - 1, file_count, half_len), jnp.bfloat16),
+            pltpu.VMEM((1, WINS * WIN), jnp.float32),
+            pltpu.VMEM((owner_count, 1, WINS * WIN), jnp.float32),
+            pltpu.VMEM((group_count, per_group, CB, LAGS), jnp.bfloat16),
+            pltpu.VMEM((group_count - 1, per_group, CB, LAGS), jnp.bfloat16),
+            pltpu.VMEM((WIN, WIN), jnp.bfloat16),
+            pltpu.VMEM((WIN, WIN), jnp.bfloat16),
+            dma((owner_count - 1,)), dma((owner_count - 1,)),
+            dma((owner_count - 1,)), dma((owner_count - 1,)),
+            dma((group_count - 1,)), dma((group_count - 1,)),
+        ],
+        compiler_params=pltpu.CompilerParams(
+            collective_id=0, has_side_effects=True, vmem_limit_bytes=48 * 1024 * 1024
+        ),
+    )(raw_files, file_target, file_len, fir_taps.reshape(1, TAPS), source_slot)
+
+
 def solution(mesh):
     placed = (P("grp", "chan", None), P("grp", "chan"), P("grp", "chan"), P(), P())
+    body = fused if mesh.shape["chan"] <= 16 else local
     return jax.shard_map(
-        local, mesh=mesh, in_specs=placed, out_specs=P("grp", "chan", None), check_vma=False
-    )
+        body, mesh=mesh, in_specs=placed, out_specs=P("grp", "chan", None), check_vma=False
+    )

time: 110 us -> 23 us (0.21)
  matrix products: 37.2 us -> 0 us
  waiting for transfers between devices: 24 us -> 0 us
  Pallas kernels: 0 us -> 18.9 us
  between operations: 15.3 us -> 0.01 us
  starting transfers between devices: 9.45 us -> 0 us
  blocking collectives: 8.35 us -> 0 us
  other arithmetic: 6.04 us -> 0 us
  local copies, waits for them, and re-layouts: 9.63 us -> 3.86 us
    conv_general_dilated x1 -> x0, matrix products: 21.9 us -> none  [decimate(): lax.conv_general_dilated(trimmed[:, None, :], kernel, (DEC,), [(TAPS - 1,...]
    reduce_scatter x1 -> x0, waiting for transfers between devices: 19.8 us -> none  [local(): lax.psum_scatter(term_rows.astype(jnp.bfloat16), 'grp', scatter_dimension...]
    pallas_call x0 -> x1, Pallas kernels: none -> 18.9 us  [fused(): pl.pallas_call(functools.partial(kernel, owner_count, group_count, stack_...]
    dot_general x17 -> x0, matrix products: 15.2 us -> none  [the longest x16 14.4 us: correlate(): lax.dot_general(window_view, shifted, (((1,), (1,)), ((), ())), preferred...]
    all_to_all x2 -> x0, starting transfers between devices: 9.41 us -> none  [the longest x1 5.2 us: local(): lax.all_to_all(ids_packed, 'chan', split_axis=0, concat_axis=0, tiled=True)]
    all_gather x1 -> x0, blocking collectives: 8.35 us -> none  [local(): lax.all_gather(own_source, 'chan', axis=0, tiled=True)]
    all_to_all x2 -> x0, waiting for transfers between devices: 4.19 us -> none  [the longest x1 4.19 us: local(): lax.all_to_all(shortened(pack_slots(filtered, 0.0)), 'chan', split_axis=0...]
    scatter x2 -> x0, local copies, waits for them, and re-layouts: 2.9 us -> none  [pack_slots(): buffer = jnp.full((slot_count,) + values.shape[1:], fill_value, values.dt...]
  transfers between devices with their start and end apart: 3 -> 0, of which waited for: 2 -> 0; matrix products, arithmetic and copies ran while one was open for 26% -> 0% of each run, Pallas kernels for 0% -> 0%
where the time goes in v1:
time: 23 us; the launch traced here: 22.8 us
  Pallas kernels  18.9 us (82%)
  local copies, waits for them, and re-layouts  3.86 us (17%)
    pallas_call x1, Pallas kernels, fused(): pl.pallas_call(functools.partial(kernel, owner_count, group_count, stack_...  18.9 us
    unnamed x11, local copies, waits for them, and re-layouts  3.86 us

profile of v1, /device:TPU:0, one launch (start us, length us, event | category | flops | bytes accessed | tf_op | source)
XLA Modules:
  0.0 22.8 jit_solution(6931774140927743588)
XLA Ops:
  0.0 0.0 copy-start.3
  0.0 0.0 copy-start.1
  0.0 0.7 %copy-done.3 = f32[64]{0:T(128)S(1)} copy-done((f32[64]{0:T(128)S(1)}, f32[64]{0:T(128)}, u32[]{:S(2)}) %copy-start.3) | copy-done | bytes 280
  0.7 0.0 copy-done.1
  0.7 0.0 copy-start
  0.7 1.2 %copy-done = f32[1,256,1024]{2,1,0:T(8,128)S(1)} copy-done((f32[1,256,1024]{2,1,0:T(8,128)S(1)}, f32[1,256,1024]{2,1,0:T(8,128)}, u32[]{:S(2)}) %copy-start) | copy-done | bytes 1048600
  1.9 0.0 copy-start.2
  1.9 0.7 %copy-done.2 = s32[1,256]{1,0:T(1,128)S(1)} copy-done((s32[1,256]{1,0:T(1,128)S(1)}, s32[1,256]{1,0:T(1,128)}, u32[]{:S(2)}) %copy-start.2) | copy-done | bytes 1048
  2.6 0.0 copy-start.4
  2.6 0.7 %copy-done.4 = s32[8]{0:T(128)S(1)} copy-done((s32[8]{0:T(128)S(1)}, s32[8]{0:T(128)}, u32[]{:S(2)}) %copy-start.4) | copy-done | bytes 56
  3.3 18.9 %shard_map.55 = bf16[2,16,256]{2,1,0:T(8,128)(2,1)S(1)} custom-call(f32[1,256,1024]{2,1,0:T(8,128)S(1)} %copy-done, s32[1,256]{1,0:T(1,128)S(1)} %copy-done.1, s32[1,256]{1,0:T(1,128)S(1)} %copy-done.2, f32[1,64]{1,0:T(1,128)S(1)} %bitcast.1, s32[8]{0:T(128)S(1)} %copy-done.4), custom_call_target="tpu_custom_call" | custom-call | tf_op jit(solution)/shard_map/pallas_call | solution.py:325
  22.2 0.6 %copy.7 = bf16[2,16,256]{2,1,0:T(8,128)(2,1)} copy(bf16[2,16,256]{2,1,0:T(8,128)(2,1)S(1)} %shard_map.55) | data formatting | bytes 32768
Async XLA Ops:
  0.0 0.7 %copy-start.3 = (f32[64]{0:T(128)S(1)}, f32[64]{0:T(128)}, u32[]{:S(2)}) copy-start(f32[64]{0:T(128)} %param.8) | copy-start | bytes 772
  0.0 0.7 %copy-start.1 = (s32[1,256]{1,0:T(1,128)S(1)}, s32[1,256]{1,0:T(1,128)}, u32[]{:S(2)}) copy-start(s32[1,256]{1,0:T(1,128)} %target_ref.1) | copy-start | bytes 3076
  0.7 1.2 %copy-start = (f32[1,256,1024]{2,1,0:T(8,128)S(1)}, f32[1,256,1024]{2,1,0:T(8,128)}, u32[]{:S(2)}) copy-start(f32[1,256,1024]{2,1,0:T(8,128)} %raw_ref.1) | copy-start | bytes 3145732
  1.9 0.7 %copy-start.2 = (s32[1,256]{1,0:T(1,128)S(1)}, s32[1,256]{1,0:T(1,128)}, u32[]{:S(2)}) copy-start(s32[1,256]{1,0:T(1,128)} %len_ref.1) | copy-start | bytes 3076
  2.6 0.7 %copy-start.4 = (s32[8]{0:T(128)S(1)}, s32[8]{0:T(128)}, u32[]{:S(2)}) copy-start(s32[8]{0:T(128)} %slot_ref.1) | copy-start | bytes 100

commit v2 on v1

--- a/solution.py
+++ b/solution.py
@@ -187,7 +187,8 @@
 
 def kernel(
     owner_count, group_count, stack_scale,
-    raw_ref, target_ref, len_ref, taps_ref, slot_ref, out_ref,
+    raw_in, target_in, len_in, taps_in, slot_in, out_ref,
+    raw_ref, target_ref, len_ref, taps_ref, slot_ref, load_sem,
     files, arrived, own_source, sources, terms, sums, band_ref, flip_ref,
     file_send, file_recv, source_send, source_recv, sum_send, sum_recv,
 ):
@@ -198,6 +199,14 @@
     per_group = owner_count // group_count
     lag_half = LAGS // 2
 
+    loads = [
+        pltpu.make_async_copy(source, landing, load_sem.at[index])
+        for index, (source, landing) in enumerate((
+            (taps_in, taps_ref), (len_in, len_ref), (raw_in, raw_ref), (target_in, target_ref), (slot_in, slot_ref),
+        ))
+    ]
+    for load in loads:
+        load.start()
     barrier = pltpu.get_barrier_semaphore()
     for step in range(1, owner_count):
         pl.semaphore_signal(
@@ -208,11 +217,14 @@
             barrier, inc=1, device_id={"grp": lax.rem(group + step, group_count)}, device_id_type=pl.DeviceIdType.MESH
         )
 
+    loads[0].wait()
+    fir_high, fir_low = split(fir_matrix(taps_ref[...]))
+    for load in loads[1:]:
+        load.wait()
     lengths = column_of(len_ref[...].astype(jnp.float32)).astype(jnp.int32)
     raw = raw_ref[0]
     trimmed = jnp.where(iota(raw.shape, 1) < lengths, raw, 0.0)
     raw_high, raw_low = split(trimmed)
-    fir_high, fir_low = split(fir_matrix(taps_ref[...]))
     filtered = dot_rows(raw_high, fir_high) + (dot_rows(raw_low, fir_high) + dot_rows(raw_high, fir_low))
     filtered = filtered.astype(jnp.bfloat16)
 
@@ -325,9 +337,15 @@
     return pl.pallas_call(
         functools.partial(kernel, owner_count, group_count, stack_scale),
         out_shape=jax.ShapeDtypeStruct((per_group, CB, LAGS), jnp.bfloat16),
-        in_specs=[vmem] * 4 + [pl.BlockSpec(memory_space=pltpu.SMEM)],
+        in_specs=[pl.BlockSpec(memory_space=pl.ANY)] * 5,
         out_specs=vmem,
         scratch_shapes=[
+            pltpu.VMEM(raw_files.shape, raw_files.dtype),
+            pltpu.VMEM(file_target.shape, file_target.dtype),
+            pltpu.VMEM(file_len.shape, file_len.dtype),
+            pltpu.VMEM((1, TAPS), fir_taps.dtype),
+            pltpu.SMEM(source_slot.shape, source_slot.dtype),
+            dma((5,)),
             pltpu.VMEM((owner_count, file_count, half_len), jnp.bfloat16),
             pltpu.VMEM((owner_count - 1, file_count, half_len), jnp.bfloat16),
             pltpu.VMEM((1, WINS * WIN), jnp.float32),
@@ -341,7 +359,7 @@
             dma((group_count - 1,)), dma((group_count - 1,)),
         ],
         compiler_params=pltpu.CompilerParams(
-            collective_id=0, has_side_effects=True, vmem_limit_bytes=48 * 1024 * 1024
+            collective_id=0, has_side_effects=True
         ),
     )(raw_files, file_target, file_len, fir_taps.reshape(1, TAPS), source_slot)
 

time: 23 us -> 20.6 us (0.90)
  local copies, waits for them, and re-layouts: 3.86 us -> 1.32 us
    unnamed x11 -> x1, local copies, waits for them, and re-layouts: 3.86 us -> 1.32 us
where the time goes in v2:
time: 20.6 us; the launch traced here: 20.4 us
  Pallas kernels  19.1 us (93%)
  local copies, waits for them, and re-layouts  1.32 us (6%)
    pallas_call x1, Pallas kernels, fused(): pl.pallas_call(functools.partial(kernel, owner_count, group_count, stack_...  19.1 us
    unnamed x1, local copies, waits for them, and re-layouts  1.32 us

profile of v2, /device:TPU:0, one launch (start us, length us, event | category | flops | bytes accessed | tf_op | source)
XLA Modules:
  0.0 20.4 jit_solution(13435093503264595202)
XLA Ops:
  0.0 19.1 %shard_map.55 = bf16[2,16,256]{2,1,0:T(8,128)(2,1)} custom-call(f32[1,256,1024]{2,1,0:T(8,128)} %raw_in.1, s32[1,256]{1,0:T(1,128)} %target_in.1, s32[1,256]{1,0:T(1,128)} %len_in.1, f32[1,64]{1,0:T(1,128)} %bitcast.1, s32[8]{0:T(128)} %slot_in.1), custom_call_target="tpu_custom_call" | custom-call | tf_op jit(solution)/shard_map/pallas_call | solution.py:337
  19.1 1.3 %copy.7 = bf16[2,16,256]{2,1,0:T(8,128)(2,1)} copy(bf16[2,16,256]{2,1,0:T(8,128)(2,1)} %shard_map.55) | data formatting | bytes 32768
